TPU v7x, 32 devices: a whole 2x2x4 slice. The times are simulated.
32 devices in a mesh: dp: 4 (over y, core), fsdp: 8 (over z, x).
Axes of the slice: x: 2, y: 2, z: 4, core: 2. Of those that a mesh axis runs over, the one named last changes fastest.
Arguments:
- hidden: bfloat16 [4096, 768], P(('dp', 'fsdp')), may hold values from -6 to 6
- memory: bfloat16 [8192, 768], P(('dp', 'fsdp')), may hold values from -6 to 6
- tgt_segments: int32 [4096], P(('dp', 'fsdp')), may hold values from 0 to 4, as said below
- mem_segments: int32 [8192], P(('dp', 'fsdp')), may hold values from 0 to 4, as said below
- labels: int32 [4096], P(('dp', 'fsdp')), may hold values from 0 to 32127
- self_query: bfloat16 [768, 768], P('fsdp', 'dp'), may hold values from -0.109375 to 0.109375
- self_key: bfloat16 [768, 768], P('fsdp', 'dp'), may hold values from -0.109375 to 0.109375
- self_value: bfloat16 [768, 768], P('fsdp', 'dp'), may hold values from -0.21875 to 0.21875
- self_out: bfloat16 [768, 768], P('fsdp', 'dp'), may hold values from -0.875 to 0.875
- cross_query: bfloat16 [768, 768], P('fsdp', 'dp'), may hold values from -0.109375 to 0.109375
- cross_key: bfloat16 [768, 768], P('fsdp', 'dp'), may hold values from -0.109375 to 0.109375
- cross_value: bfloat16 [768, 768], P('fsdp', 'dp'), may hold values from -0.21875 to 0.21875
- cross_out: bfloat16 [768, 768], P('fsdp', 'dp'), may hold values from -0.875 to 0.875
- gate_weight: bfloat16 [768, 2048], P('fsdp', 'dp'), may hold values from -0.21875 to 0.21875
- up_weight: bfloat16 [768, 2048], P('fsdp', 'dp'), may hold values from -0.21875 to 0.21875
- down_weight: bfloat16 [2048, 768], P('fsdp', 'dp'), may hold values from -0.25 to 0.25
- norm_gains: bfloat16 [3072], P(('dp', 'fsdp')), may hold values from 0.5 to 1.5
- embedding: bfloat16 [32128, 768], P('fsdp', 'dp'), may hold values from -12 to 12
Outputs:
- block_out: bfloat16 [4096, 768], P(('dp', 'fsdp'))
- loss_mean: float32 [], replicated
- grad_hidden: float32 [4096, 768], P(('dp', 'fsdp'))
- grad_memory: float32 [8192, 768], P(('dp', 'fsdp'))
- grad_self_query: float32 [768, 768], P('fsdp', 'dp')
- grad_self_key: float32 [768, 768], P('fsdp', 'dp')
- grad_self_value: float32 [768, 768], P('fsdp', 'dp')
- grad_self_out: float32 [768, 768], P('fsdp', 'dp')
- grad_cross_query: float32 [768, 768], P('fsdp', 'dp')
- grad_cross_key: float32 [768, 768], P('fsdp', 'dp')
- grad_cross_value: float32 [768, 768], P('fsdp', 'dp')
- grad_cross_out: float32 [768, 768], P('fsdp', 'dp')
- grad_gate: float32 [768, 2048], P('fsdp', 'dp')
- grad_up: float32 [768, 2048], P('fsdp', 'dp')
- grad_down: float32 [2048, 768], P('fsdp', 'dp')
- grad_gains: float32 [3072], P(('dp', 'fsdp'))
- grad_embedding: float32 [32128, 768], P('fsdp', 'dp')
Inputs may be any that keep to these rules, and one draw needn't show every extreme that they name: `tgt_segments`: in each row of 128 target tokens the valid tokens come first and hold examples 1 to 4 in order, each non-empty; the row ends with one or more padding tokens marked 0. `mem_segments`: in each row of 256 memory tokens (row r serves target row r) the valid tokens come first and hold examples 1 to 4 in order, each non-empty; the row ends with one or more padding tokens marked 0.
All inputs are finite; a program needn't handle non-finite values.
Results may differ from a plain program's by a relative error of at most 0.03.
The roundings to bfloat16 on the way count: a program that leaves them out, or rounds other values in their place, can miss the bound.
Values may be sent and summed in bfloat16 or wider, within the bound.
No kernel may reach another device: no remote copies, remote signals or barrier semaphores. Data moves between devices by JAX's collectives and lax.ppermute only.
A program may use at most 320 MiB of HBM per device.

v0:
```python
import jax
import jax.numpy as jnp
from jax import lax
from jax.sharding import PartitionSpec as P

D = 768
HEADS = 12
HEAD_DIM = 64


EPS = 1e-06
NEG = -1e30


def normalize(values):
    return values * lax.rsqrt(jnp.mean(values * values, axis=-1, keepdims=True) + EPS)


def norm_back(values, gain, grad, factor):

    def scaled(inner, weight):
        return normalize(inner) * weight * factor

    _, pull = jax.vjp(scaled, values, gain)
    return pull(grad)


def matmul(left, right):
    return jnp.dot(left, right, preferred_element_type=jnp.float32)


def times_transposed(left, right):
    return lax.dot_general(
        left, right, (((1,), (1,)), ((), ())), preferred_element_type=jnp.float32
    )


def transposed_times(left, right):
    return lax.dot_general(
        left, right, (((0,), (0,)), ((), ())), preferred_element_type=jnp.float32
    )


def split_heads(values):
    return values.reshape(values.shape[0], HEADS, HEAD_DIM)


def join_heads(values):
    return values.reshape(values.shape[0], HEADS * HEAD_DIM)


def masked_scores(query, keys, mask):
    scores = jnp.einsum(
        "thd,shd->hts", split_heads(query), split_heads(keys), preferred_element_type=jnp.float32
    )
    return jnp.where(mask[None], scores, NEG)


def attend(query, keys, values, mask):
    scores = masked_scores(query, keys, mask)
    top = jnp.max(scores, axis=-1, keepdims=True)
    normalizer = top + jnp.log(jnp.sum(jnp.exp(scores - top), axis=-1, keepdims=True))
    shares = jnp.exp(scores - normalizer).astype(jnp.bfloat16)
    mixed = jnp.einsum(
        "hts,shd->thd", shares, split_heads(values), preferred_element_type=jnp.float32
    )
    return (join_heads(mixed).astype(jnp.bfloat16), normalizer)


def attend_back(query, keys, values, mask, normalizer, out_grad):
    shares = jnp.exp(masked_scores(query, keys, mask) - normalizer)
    heads_grad = split_heads(out_grad)
    share_grad = jnp.einsum(
        "thd,shd->hts", heads_grad, split_heads(values), preferred_element_type=jnp.float32
    )
    inner = jnp.sum(shares * share_grad, axis=-1, keepdims=True)
    score_grad = (shares * (share_grad - inner)).astype(jnp.bfloat16)
    query_grad = jnp.einsum(
        "hts,shd->thd", score_grad, split_heads(keys), preferred_element_type=jnp.float32
    )
    key_grad = jnp.einsum(
        "hts,thd->shd", score_grad, split_heads(query), preferred_element_type=jnp.float32
    )
    value_grad = jnp.einsum(
        "hts,thd->shd", shares.astype(jnp.bfloat16), heads_grad, preferred_element_type=jnp.float32
    )
    return (
        join_heads(query_grad).astype(jnp.bfloat16),
        join_heads(key_grad).astype(jnp.bfloat16),
        join_heads(value_grad).astype(jnp.bfloat16),
    )


def body(
    hidden,
    memory,
    tgt_segments,
    mem_segments,
    labels,
    self_query,
    self_key,
    self_value,
    self_out,
    cross_query,
    cross_key,
    cross_value,
    cross_out,
    gate_weight,
    up_weight,
    down_weight,
    norm_gains,
    embedding,
):
    table_local = lax.all_gather(embedding, "dp", axis=1, tiled=True)
    pieces = (
        lax.all_gather(self_query, "fsdp", axis=0, tiled=True),
        lax.all_gather(self_key, "fsdp", axis=0, tiled=True),
        lax.all_gather(self_value, "fsdp", axis=0, tiled=True),
        lax.all_gather(self_out, "fsdp", axis=0, tiled=True),
        lax.all_gather(cross_query, "fsdp", axis=0, tiled=True),
        lax.all_gather(cross_key, "fsdp", axis=0, tiled=True),
        lax.all_gather(cross_value, "fsdp", axis=0, tiled=True),
        lax.all_gather(cross_out, "fsdp", axis=0, tiled=True),
        lax.all_gather(gate_weight, "fsdp", axis=0, tiled=True),
        lax.all_gather(up_weight, "fsdp", axis=0, tiled=True),
        lax.all_gather(down_weight, "fsdp", axis=0, tiled=True),
        lax.all_gather(table_local, "fsdp", axis=0, tiled=True),
    )
    table_full = pieces[11]
    whole = (
        lax.all_gather(pieces[0], "dp", axis=1, tiled=True),
        lax.all_gather(pieces[1], "dp", axis=1, tiled=True),
        lax.all_gather(pieces[2], "dp", axis=1, tiled=True),
        lax.all_gather(pieces[3], "dp", axis=1, tiled=True),
        lax.all_gather(pieces[4], "dp", axis=1, tiled=True),
        lax.all_gather(pieces[5], "dp", axis=1, tiled=True),
        lax.all_gather(pieces[6], "dp", axis=1, tiled=True),
        lax.all_gather(pieces[7], "dp", axis=1, tiled=True),
        lax.all_gather(pieces[8], "dp", axis=1, tiled=True),
        lax.all_gather(pieces[9], "dp", axis=1, tiled=True),
        lax.all_gather(pieces[10], "dp", axis=1, tiled=True),
    )
    (
        query_full,
        key_full,
        value_full,
        output_full,
        recall_query,
        recall_key,
        recall_value,
        recall_output,
        gate_full,
        up_full,
        down_full,
    ) = whole
    gains = (
        lax.all_gather(norm_gains, ("dp", "fsdp"), axis=0, tiled=True)
        .astype(jnp.float32)
        .reshape(4, -1)
    )
    inputs = hidden.astype(jnp.float32)
    length = hidden.shape[0]
    places = jnp.arange(length)
    self_mask = (tgt_segments[:, None] == tgt_segments[None, :]) & (
        places[None, :] <= places[:, None]
    )
    cross_mask = (tgt_segments[:, None] == mem_segments[None, :]) | (tgt_segments[:, None] == 0)
    valid = (tgt_segments > 0).astype(jnp.float32)
    first_normed = (normalize(inputs) * gains[0]).astype(jnp.bfloat16)
    queries = matmul(first_normed, query_full).astype(jnp.bfloat16)
    keys = matmul(first_normed, key_full).astype(jnp.bfloat16)
    values = matmul(first_normed, value_full).astype(jnp.bfloat16)
    attended, self_norms = attend(queries, keys, values, self_mask)
    after_self = inputs + matmul(attended, output_full)
    second_normed = (normalize(after_self) * gains[1]).astype(jnp.bfloat16)
    asked = matmul(second_normed, recall_query).astype(jnp.bfloat16)
    memory_keys = matmul(memory, recall_key).astype(jnp.bfloat16)
    memory_values = matmul(memory, recall_value).astype(jnp.bfloat16)
    recalled, cross_norms = attend(asked, memory_keys, memory_values, cross_mask)
    after_cross = after_self + matmul(recalled, recall_output)
    third_normed = (normalize(after_cross) * gains[2]).astype(jnp.bfloat16)
    gate_rows = matmul(third_normed, gate_full)
    up_rows = matmul(third_normed, up_full)
    activated = (jax.nn.gelu(gate_rows, approximate=True) * up_rows).astype(jnp.bfloat16)
    block_sum = after_cross + matmul(activated, down_full)
    exit_rows = (normalize(block_sum) * gains[3] * D ** (-0.5)).astype(jnp.bfloat16)
    logits = times_transposed(exit_rows, table_full)
    top = jnp.max(logits, axis=1, keepdims=True)
    normalizer = top + jnp.log(jnp.sum(jnp.exp(logits - top), axis=1, keepdims=True))
    onehot = (jnp.arange(logits.shape[1])[None, :] == labels[:, None]).astype(jnp.float32)
    picked = jnp.sum(onehot * logits, axis=1)
    local_loss = jnp.sum((normalizer[:, 0] - picked) * valid)
    logit_grad = ((jnp.exp(logits - normalizer) - onehot) * valid[:, None]).astype(jnp.bfloat16)
    exit_grad = matmul(logit_grad, table_full)
    vocab_rows = lax.psum_scatter(
        transposed_times(logit_grad, exit_rows).astype(jnp.bfloat16),
        "fsdp",
        scatter_dimension=0,
        tiled=True,
    )
    grad_embedding = lax.psum_scatter(vocab_rows, "dp", scatter_dimension=1, tiled=True).astype(
        jnp.float32
    )
    block_grad, exit_gain = norm_back(block_sum, gains[3], exit_grad, D ** (-0.5))
    again = (
        lax.all_gather(self_query, "fsdp", axis=0, tiled=True),
        lax.all_gather(self_key, "fsdp", axis=0, tiled=True),
        lax.all_gather(self_value, "fsdp", axis=0, tiled=True),
        lax.all_gather(self_out, "fsdp", axis=0, tiled=True),
        lax.all_gather(cross_query, "fsdp", axis=0, tiled=True),
        lax.all_gather(cross_key, "fsdp", axis=0, tiled=True),
        lax.all_gather(cross_value, "fsdp", axis=0, tiled=True),
        lax.all_gather(cross_out, "fsdp", axis=0, tiled=True),
        lax.all_gather(gate_weight, "fsdp", axis=0, tiled=True),
        lax.all_gather(up_weight, "fsdp", axis=0, tiled=True),
        lax.all_gather(down_weight, "fsdp", axis=0, tiled=True),
    )
    layer = (
        lax.all_gather(again[0], "dp", axis=1, tiled=True),
        lax.all_gather(again[1], "dp", axis=1, tiled=True),
        lax.all_gather(again[2], "dp", axis=1, tiled=True),
        lax.all_gather(again[3], "dp", axis=1, tiled=True),
        lax.all_gather(again[4], "dp", axis=1, tiled=True),
        lax.all_gather(again[5], "dp", axis=1, tiled=True),
        lax.all_gather(again[6], "dp", axis=1, tiled=True),
        lax.all_gather(again[7], "dp", axis=1, tiled=True),
        lax.all_gather(again[8], "dp", axis=1, tiled=True),
        lax.all_gather(again[9], "dp", axis=1, tiled=True),
        lax.all_gather(again[10], "dp", axis=1, tiled=True),
    )
    (
        query_full,
        key_full,
        value_full,
        output_full,
        recall_query,
        recall_key,
        recall_value,
        recall_output,
        gate_full,
        up_full,
        down_full,
    ) = layer
    down_input = block_grad.astype(jnp.bfloat16)
    grad_down = transposed_times(activated, down_input)
    act_grad = times_transposed(down_input, down_full)
    _, pull = jax.vjp(
        lambda gate_in, up_in: jax.nn.gelu(gate_in, approximate=True) * up_in, gate_rows, up_rows
    )
    gate_grad, up_grad = pull(act_grad)
    gate_grad = gate_grad.astype(jnp.bfloat16)
    up_grad = up_grad.astype(jnp.bfloat16)
    grad_gate = transposed_times(third_normed, gate_grad)
    grad_up = transposed_times(third_normed, up_grad)
    third_grad = times_transposed(gate_grad, gate_full) + times_transposed(up_grad, up_full)
    cross_back, third_gain = norm_back(after_cross, gains[2], third_grad, 1.0)
    after_cross_grad = block_grad + cross_back
    cross_branch = after_cross_grad.astype(jnp.bfloat16)
    grad_cross_out = transposed_times(recalled, cross_branch)
    recalled_grad = times_transposed(cross_branch, recall_output).astype(jnp.bfloat16)
    probe_grad, lookup_grad, content_grad = attend_back(
        asked, memory_keys, memory_values, cross_mask, cross_norms, recalled_grad
    )
    grad_cross_query = transposed_times(second_normed, probe_grad)
    grad_cross_key = transposed_times(memory, lookup_grad)
    grad_cross_value = transposed_times(memory, content_grad)
    grad_memory = times_transposed(lookup_grad, recall_key) + times_transposed(
        content_grad, recall_value
    )
    second_grad = times_transposed(probe_grad, recall_query)
    self_back, second_gain = norm_back(after_self, gains[1], second_grad, 1.0)
    after_self_grad = after_cross_grad + self_back
    self_branch = after_self_grad.astype(jnp.bfloat16)
    grad_self_out = transposed_times(attended, self_branch)
    attended_grad = times_transposed(self_branch, output_full).astype(jnp.bfloat16)
    query_grad, key_grad, value_grad = attend_back(
        queries, keys, values, self_mask, self_norms, attended_grad
    )
    grad_self_query = transposed_times(first_normed, query_grad)
    grad_self_key = transposed_times(first_normed, key_grad)
    grad_self_value = transposed_times(first_normed, value_grad)
    first_grad = (
        times_transposed(query_grad, query_full)
        + times_transposed(key_grad, key_full)
        + times_transposed(value_grad, value_full)
    )
    input_back, first_gain = norm_back(inputs, gains[0], first_grad, 1.0)
    grad_hidden = after_self_grad + input_back
    columns = (
        lax.psum_scatter(
            grad_self_query.astype(jnp.bfloat16), "dp", scatter_dimension=1, tiled=True
        ).astype(jnp.float32),
        lax.psum_scatter(
            grad_self_key.astype(jnp.bfloat16), "dp", scatter_dimension=1, tiled=True
        ).astype(jnp.float32),
        lax.psum_scatter(
            grad_self_value.astype(jnp.bfloat16), "dp", scatter_dimension=1, tiled=True
        ).astype(jnp.float32),
        lax.psum_scatter(
            grad_self_out.astype(jnp.bfloat16), "dp", scatter_dimension=1, tiled=True
        ).astype(jnp.float32),
        lax.psum_scatter(
            grad_cross_query.astype(jnp.bfloat16), "dp", scatter_dimension=1, tiled=True
        ).astype(jnp.float32),
        lax.psum_scatter(
            grad_cross_key.astype(jnp.bfloat16), "dp", scatter_dimension=1, tiled=True
        ).astype(jnp.float32),
        lax.psum_scatter(
            grad_cross_value.astype(jnp.bfloat16), "dp", scatter_dimension=1, tiled=True
        ).astype(jnp.float32),
        lax.psum_scatter(
            grad_cross_out.astype(jnp.bfloat16), "dp", scatter_dimension=1, tiled=True
        ).astype(jnp.float32),
        lax.psum_scatter(
            grad_gate.astype(jnp.bfloat16), "dp", scatter_dimension=1, tiled=True
        ).astype(jnp.float32),
        lax.psum_scatter(
            grad_up.astype(jnp.bfloat16), "dp", scatter_dimension=1, tiled=True
        ).astype(jnp.float32),
        lax.psum_scatter(
            grad_down.astype(jnp.bfloat16), "dp", scatter_dimension=1, tiled=True
        ).astype(jnp.float32),
    )
    owned = (
        lax.psum_scatter(
            columns[0].astype(jnp.bfloat16), "fsdp", scatter_dimension=0, tiled=True
        ).astype(jnp.float32),
        lax.psum_scatter(
            columns[1].astype(jnp.bfloat16), "fsdp", scatter_dimension=0, tiled=True
        ).astype(jnp.float32),
        lax.psum_scatter(
            columns[2].astype(jnp.bfloat16), "fsdp", scatter_dimension=0, tiled=True
        ).astype(jnp.float32),
        lax.psum_scatter(
            columns[3].astype(jnp.bfloat16), "fsdp", scatter_dimension=0, tiled=True
        ).astype(jnp.float32),
        lax.psum_scatter(
            columns[4].astype(jnp.bfloat16), "fsdp", scatter_dimension=0, tiled=True
        ).astype(jnp.float32),
        lax.psum_scatter(
            columns[5].astype(jnp.bfloat16), "fsdp", scatter_dimension=0, tiled=True
        ).astype(jnp.float32),
        lax.psum_scatter(
            columns[6].astype(jnp.bfloat16), "fsdp", scatter_dimension=0, tiled=True
        ).astype(jnp.float32),
        lax.psum_scatter(
            columns[7].astype(jnp.bfloat16), "fsdp", scatter_dimension=0, tiled=True
        ).astype(jnp.float32),
        lax.psum_scatter(
            columns[8].astype(jnp.bfloat16), "fsdp", scatter_dimension=0, tiled=True
        ).astype(jnp.float32),
        lax.psum_scatter(
            columns[9].astype(jnp.bfloat16), "fsdp", scatter_dimension=0, tiled=True
        ).astype(jnp.float32),
        lax.psum_scatter(
            columns[10].astype(jnp.bfloat16), "fsdp", scatter_dimension=0, tiled=True
        ).astype(jnp.float32),
    )
    gain_grad = lax.psum_scatter(
        jnp.concatenate([first_gain, second_gain, third_gain, exit_gain]),
        ("dp", "fsdp"),
        scatter_dimension=0,
        tiled=True,
    )
    loss_total = lax.psum(local_loss, ("dp", "fsdp"))
    loss_mean = loss_total / (length * lax.axis_size("dp") * lax.axis_size("fsdp"))
    return (
        block_sum.astype(jnp.bfloat16),
        loss_mean,
        grad_hidden,
        grad_memory,
        owned[0],
        owned[1],
        owned[2],
        owned[3],
        owned[4],
        owned[5],
        owned[6],
        owned[7],
        owned[8],
        owned[9],
        owned[10],
        gain_grad,
        grad_embedding,
    )


def solution(mesh):
    in_specs = (
        P(("dp", "fsdp"), None),
        P(("dp", "fsdp"), None),
        P(("dp", "fsdp")),
        P(("dp", "fsdp")),
        P(("dp", "fsdp")),
        P("fsdp", "dp"),
        P("fsdp", "dp"),
        P("fsdp", "dp"),
        P("fsdp", "dp"),
        P("fsdp", "dp"),
        P("fsdp", "dp"),
        P("fsdp", "dp"),
        P("fsdp", "dp"),
        P("fsdp", "dp"),
        P("fsdp", "dp"),
        P("fsdp", "dp"),
        P(("dp", "fsdp")),
        P("fsdp", "dp"),
    )
    out_specs = (
        P(("dp", "fsdp"), None),
        P(),
        P(("dp", "fsdp"), None),
        P(("dp", "fsdp"), None),
        P("fsdp", "dp"),
        P("fsdp", "dp"),
        P("fsdp", "dp"),
        P("fsdp", "dp"),
        P("fsdp", "dp"),
        P("fsdp", "dp"),
        P("fsdp", "dp"),
        P("fsdp", "dp"),
        P("fsdp", "dp"),
        P("fsdp", "dp"),
        P("fsdp", "dp"),
        P(("dp", "fsdp")),
        P("fsdp", "dp"),
    )
    return jax.shard_map(body, mesh=mesh, in_specs=in_specs, out_specs=out_specs, check_vma=False)
```

profile of v0, /device:TPU:0, one launch (start us, length us, event | category | flops | bytes accessed | tf_op | source)
XLA Modules:
  0.0 3329.9 jit_solution(5386060167874736874)
XLA Ops:
  8.1 32.8 all_gather.98
  41.8 31.1 all_gather.100
  73.8 31.0 all_gather.102
  105.7 31.0 all_gather.106
  137.7 31.3 all_gather.104
  169.9 31.0 all_gather.108
  201.9 31.1 all_gather.110
  234.0 31.2 all_gather.112
  266.1 34.2 %all_gather.114 = bf16[768,512]{1,0:T(8,128)(2,1)} all-gather(bf16[96,512]{1,0:T(8,128)(2,1)S(1)} %copy-done.55), channel_id=1, replica_groups=mesh['dp'=4,'fsdp'=8] {'fsdp'}, dimensions={0}, use_global_device_ids=true | all-gather | bytes 884736 | tf_op jit(solution)/shard_map/all_gather | solution.py:124
  300.4 33.6 %all_gather.116 = bf16[768,512]{1,0:T(8,128)(2,1)} all-gather(bf16[96,512]{1,0:T(8,128)(2,1)S(1)} %copy-done.56), channel_id=1, replica_groups=mesh['dp'=4,'fsdp'=8] {'fsdp'}, dimensions={0}, use_global_device_ids=true | all-gather | bytes 884736 | tf_op jit(solution)/shard_map/all_gather | solution.py:125
  334.1 33.6 %all_gather.118 = bf16[2048,192]{0,1:T(8,128)(2,1)} all-gather(bf16[256,192]{0,1:T(8,128)(2,1)S(1)} %copy-done.57), channel_id=1, replica_groups=mesh['dp'=4,'fsdp'=8] {'fsdp'}, dimensions={0}, use_global_device_ids=true | all-gather | bytes 884736 | tf_op jit(solution)/shard_map/all_gather | solution.py:126
  367.9 8.7 copy.130
  377.4 105.7 %all-reduce = bf16[3072]{0:T(1024)(128)(2,1)S(1)} all-reduce(bf16[3072]{0:T(1024)(128)(2,1)S(1)} %dynamic-update-slice), channel_id=1, replica_groups=mesh['dp'=4,'fsdp'=8] {'dp','fsdp'}, use_global_device_ids=true, to_apply=%add | all-reduce | flops 3072 | bytes 12288
  507.9 3.4 fusion.49
  511.4 4.2 multiply_convert_fusion.3
  515.5 4.0 multiply_reduce_fusion.8
  520.6 814.1 %all-gather.38.cloned.1.call-done = bf16[32128,768]{1,0:T(8,128)(2,1)} async-done(((bf16[4016,768]{1,0:T(8,128)(2,1)}), bf16[32128,768]{1,0:T(8,128)(2,1)}) %all-gather.38.cloned.1.call-update) | async-done | bytes 49348624 | tf_op jit(solution)/shard_map/all_gather | solution.py:127
  1334.7 27.2 fusion.48
  1361.9 9.3 select_reduce_fusion
  1371.9 24.7 multiply_reduce_fusion.2
  1398.3 3.7 multiply_convert_fusion.2
  1454.6 25.4 convolution_convert_fusion
  1484.1 21.0 reduce-scatter.49.cloned.1.call-done
  1507.0 26.1 reduce-scatter.51.cloned.1.call-done
  1535.1 26.1 reduce-scatter.53.cloned.1.call-done
  1563.1 26.2 reduce-scatter.55.cloned.1.call-done
  1591.3 26.1 reduce-scatter.57.cloned.1.call-done
  1619.3 26.2 reduce-scatter.59.cloned.1.call-done
  1647.5 38.9 %reduce-scatter.61.cloned.1.call-done = bf16[768,512]{1,0:T(8,128)(2,1)} async-done(((bf16[768,2048]{1,0:T(8,128)(2,1)}), bf16[768,512]{1,0:T(8,128)(2,1)}) %reduce-scatter.61.cloned.1.call-update) | async-done | bytes 786448 | tf_op jit(solution)/shard_map/reduce_scatter | solution.py:314
  1686.6 40.1 %reduce-scatter.65.cloned.1.call-done = bf16[768,512]{1,0:T(8,128)(2,1)} async-done(((bf16[768,2048]{1,0:T(8,128)(2,1)}), bf16[768,512]{1,0:T(8,128)(2,1)}) %reduce-scatter.65.cloned.1.call-update) | async-done | bytes 786448 | tf_op jit(solution)/shard_map/reduce_scatter | solution.py:317
  1726.7 40.2 %reduce-scatter.69.cloned.1.call-done = bf16[2048,192]{0,1:T(8,128)(2,1)} async-done(((bf16[2048,768]{0,1:T(8,128)(2,1)}), bf16[2048,192]{0,1:T(8,128)(2,1)}) %reduce-scatter.69.cloned.1.call-update) | async-done | bytes 786448 | tf_op jit(solution)/shard_map/reduce_scatter | solution.py:320
  1767.0 775.3 %reduce-scatter.91.cloned.1.call-done = bf16[4016,768]{1,0:T(8,128)(2,1)} async-done(((bf16[32128,768]{1,0:T(8,128)(2,1)}), bf16[4016,768]{1,0:T(8,128)(2,1)}) %reduce-scatter.91.cloned.1.call-update) | async-done | bytes 6168592
  2542.4 8.6 copy.165
  2554.8 39.5 %all-reduce.3 = (f32[]{:T(128)}, f32[3072]{0:T(1024)S(1)}) all-reduce(f32[]{:T(128)} %get-tuple-element.97, f32[3072]{0:T(1024)S(1)} %pad_maximum_fusion), channel_id=1, replica_groups=mesh['dp'=4,'fsdp'=8] {'dp','fsdp'}, use_global_device_ids=true, to_apply=%region_12.13 | all-reduce | flops 3073 | bytes 24584 | tf_op jit(solution)/shard_map/psum | solution.py:365
  2598.4 8.5 reduce-scatter.73.cloned.1.call-done
  2608.6 62.8 %reduce-scatter.75.cloned.1.call-done = bf16[96,192]{1,0:T(8,128)(2,1)} async-done(((bf16[768,192]{1,0:T(8,128)(2,1)}), bf16[96,192]{1,0:T(8,128)(2,1)}) %reduce-scatter.75.cloned.1.call-update) | async-done | bytes 36880
  2673.0 62.8 %reduce-scatter.77.cloned.1.call-done = bf16[96,192]{1,0:T(8,128)(2,1)} async-done(((bf16[768,192]{1,0:T(8,128)(2,1)}), bf16[96,192]{1,0:T(8,128)(2,1)}) %reduce-scatter.77.cloned.1.call-update) | async-done | bytes 36880
  2737.4 62.8 %reduce-scatter.79.cloned.1.call-done = bf16[96,192]{1,0:T(8,128)(2,1)} async-done(((bf16[768,192]{1,0:T(8,128)(2,1)}), bf16[96,192]{1,0:T(8,128)(2,1)}) %reduce-scatter.79.cloned.1.call-update) | async-done | bytes 36880
  2801.9 62.6 %reduce-scatter.81.cloned.1.call-done = bf16[96,192]{1,0:T(8,128)(2,1)} async-done(((bf16[768,192]{1,0:T(8,128)(2,1)}), bf16[96,192]{1,0:T(8,128)(2,1)}) %reduce-scatter.81.cloned.1.call-update) | async-done | bytes 36880
  2866.2 62.8 %reduce-scatter.83.cloned.1.call-done = bf16[96,192]{1,0:T(8,128)(2,1)} async-done(((bf16[768,192]{1,0:T(8,128)(2,1)}), bf16[96,192]{1,0:T(8,128)(2,1)}) %reduce-scatter.83.cloned.1.call-update) | async-done | bytes 36880
  2930.6 62.8 %reduce-scatter.85.cloned.1.call-done = bf16[96,192]{1,0:T(8,128)(2,1)} async-done(((bf16[768,192]{1,0:T(8,128)(2,1)}), bf16[96,192]{1,0:T(8,128)(2,1)}) %reduce-scatter.85.cloned.1.call-update) | async-done | bytes 36880
  2995.1 62.7 %reduce-scatter.87.cloned.1.call-done = bf16[96,192]{1,0:T(8,128)(2,1)} async-done(((bf16[768,192]{1,0:T(8,128)(2,1)}), bf16[96,192]{1,0:T(8,128)(2,1)}) %reduce-scatter.87.cloned.1.call-update) | async-done | bytes 36880
  3059.5 64.0 %reduce-scatter.63.cloned.1.call-done = bf16[96,512]{1,0:T(8,128)(2,1)} async-done(((bf16[768,512]{1,0:T(8,128)(2,1)}), bf16[96,512]{1,0:T(8,128)(2,1)}) %reduce-scatter.63.cloned.1.call-update) | async-done | bytes 98320 | tf_op jit(solution)/shard_map/reduce_scatter | solution.py:349
  3125.1 64.1 %reduce-scatter.67.cloned.1.call-done = bf16[96,512]{1,0:T(8,128)(2,1)} async-done(((bf16[768,512]{1,0:T(8,128)(2,1)}), bf16[96,512]{1,0:T(8,128)(2,1)}) %reduce-scatter.67.cloned.1.call-update) | async-done | bytes 98320 | tf_op jit(solution)/shard_map/reduce_scatter | solution.py:352
  3190.7 64.6 %reduce-scatter.71.cloned.1.call-done = bf16[256,192]{0,1:T(8,128)(2,1)} async-done(((bf16[2048,192]{0,1:T(8,128)(2,1)}), bf16[256,192]{0,1:T(8,128)(2,1)}) %reduce-scatter.71.cloned.1.call-update) | async-done | bytes 98320 | tf_op jit(solution)/shard_map/reduce_scatter | solution.py:355
  3256.9 58.7 %reduce-scatter.89.cloned.1.call-done = bf16[192,4016]{1,0:T(8,128)(2,1)} async-done(((bf16[768,4016]{1,0:T(8,128)(2,1)}), bf16[192,4016]{1,0:T(8,128)(2,1)}) %reduce-scatter.89.cloned.1.call-update) | async-done | bytes 1542160
  3315.6 3.1 copy.166
  3318.7 3.1 copy.144
  (405 shorter events, 130.1 us)
Async XLA Ops:
  7.2 484.8 %copy-start = (bf16[256,768]{1,0:T(8,128)(2,1)S(1)}, bf16[256,768]{1,0:T(8,128)(2,1)}, u32[]{:S(2)}) copy-start(bf16[256,768]{1,0:T(8,128)(2,1)} %param.19) | copy-start | bytes 1179652
  7.2 360.6 %all-gather.36.cloned.1.call-start = ((), (), s32[]{:S(2)}) async-start(), calls=%async_computation.35 | async-start | bytes 7864320 | tf_op jit(solution)/shard_map/all_gather | solution.py:114
  8.0 65.8 %copy-start.62 = (bf16[96,192]{1,0:T(8,128)(2,1)S(1)}, bf16[96,192]{1,0:T(8,128)(2,1)}, u32[]{:S(2)}) copy-start(bf16[96,192]{1,0:T(8,128)(2,1)} %param.24) | copy-start | bytes 110596
  8.0 477.8 %all-gather.14.cloned.1.call-start = ((), (), s32[]{:S(2)}) async-start(), calls=%async_computation.24 | async-start | bytes 1474560 | tf_op jit(solution)/shard_map/all_gather | solution.py:133
  41.7 446.1 %all-gather.16.cloned.1.call-start = ((), (), s32[]{:S(2)}) async-start(), calls=%async_computation.25 | async-start | bytes 1474560 | tf_op jit(solution)/shard_map/all_gather | solution.py:131
  73.7 416.2 %all-gather.18.cloned.1.call-start = ((), (), s32[]{:S(2)}) async-start(), calls=%async_computation.26 | async-start | bytes 1474560 | tf_op jit(solution)/shard_map/all_gather | solution.py:132
  105.6 64.3 %copy-start.65 = (bf16[96,192]{1,0:T(8,128)(2,1)S(1)}, bf16[96,192]{1,0:T(8,128)(2,1)}, u32[]{:S(2)}) copy-start(bf16[96,192]{1,0:T(8,128)(2,1)} %param.27) | copy-start | bytes 110596
  105.7 386.3 %all-gather.22.cloned.1.call-start = ((), (), s32[]{:S(2)}) async-start(), calls=%async_computation.28 | async-start | bytes 1474560 | tf_op jit(solution)/shard_map/all_gather | solution.py:137
  137.6 64.3 %copy-start.66 = (bf16[96,192]{1,0:T(8,128)(2,1)S(1)}, bf16[96,192]{1,0:T(8,128)(2,1)}, u32[]{:S(2)}) copy-start(bf16[96,192]{1,0:T(8,128)(2,1)} %param.28) | copy-start | bytes 110596
  137.6 357.9 %all-gather.20.cloned.1.call-start = ((), (), s32[]{:S(2)}) async-start(), calls=%async_computation.27 | async-start | bytes 1474560 | tf_op jit(solution)/shard_map/all_gather | solution.py:134
  169.9 64.1 %copy-start.67 = (bf16[96,192]{1,0:T(8,128)(2,1)S(1)}, bf16[96,192]{1,0:T(8,128)(2,1)}, u32[]{:S(2)}) copy-start(bf16[96,192]{1,0:T(8,128)(2,1)} %param.30) | copy-start | bytes 110596
  169.9 327.7 %all-gather.24.cloned.1.call-start = ((), (), s32[]{:S(2)}) async-start(), calls=%async_computation.29 | async-start | bytes 1474560 | tf_op jit(solution)/shard_map/all_gather | solution.py:135
  201.8 64.3 %copy-start.55 = (bf16[96,512]{1,0:T(8,128)(2,1)S(1)}, bf16[96,512]{1,0:T(8,128)(2,1)}, u32[]{:S(2)}) copy-start(bf16[96,512]{1,0:T(8,128)(2,1)} %param.31) | copy-start | bytes 294916
  201.8 297.8 %all-gather.26.cloned.1.call-start = ((), (), s32[]{:S(2)}) async-start(), calls=%async_computation.30 | async-start | bytes 1474560 | tf_op jit(solution)/shard_map/all_gather | solution.py:136
  233.9 66.5 %copy-start.56 = (bf16[96,512]{1,0:T(8,128)(2,1)S(1)}, bf16[96,512]{1,0:T(8,128)(2,1)}, u32[]{:S(2)}) copy-start(bf16[96,512]{1,0:T(8,128)(2,1)} %param.32) | copy-start | bytes 294916
  233.9 271.1 %all-gather.28.cloned.1.call-start = ((), (), s32[]{:S(2)}) async-start(), calls=%async_computation.31 | async-start | bytes 1474560 | tf_op jit(solution)/shard_map/all_gather | solution.py:138
  266.0 68.1 %copy-start.57 = (bf16[256,192]{0,1:T(8,128)(2,1)S(1)}, bf16[256,192]{0,1:T(8,128)(2,1)}, u32[]{:S(2)}) copy-start(bf16[256,192]{0,1:T(8,128)(2,1)} %param.33) | copy-start | bytes 294916
  266.1 241.9 %all-gather.30.cloned.1.call-start = ((), (), s32[]{:S(2)}) async-start(), calls=%async_computation.32 | async-start | bytes 3932160 | tf_op jit(solution)/shard_map/all_gather | solution.py:139
  300.4 211.0 %all-gather.32.cloned.1.call-start = ((), (), s32[]{:S(2)}) async-start(), calls=%async_computation.33 | async-start | bytes 3932160 | tf_op jit(solution)/shard_map/all_gather | solution.py:140
  334.1 181.5 %all-gather.34.cloned.1.call-start = ((), (), s32[]{:S(2)}) async-start(), calls=%async_computation.34 | async-start | bytes 3932160 | tf_op jit(solution)/shard_map/all_gather | solution.py:141
  367.8 966.9 %all-gather.38.cloned.1.call-start = ((), (), s32[]{:S(2)}) async-start(), calls=%async_computation.36 | async-start | bytes 55517184 | tf_op jit(solution)/shard_map/all_gather | solution.py:127
  376.5 106.6 %copy-start.1 = (bf16[128,768]{1,0:T(8,128)(2,1)S(1)}, bf16[128,768]{1,0:T(8,128)(2,1)}, u32[]{:S(2)}) copy-start(bf16[128,768]{1,0:T(8,128)(2,1)} %param.18) | copy-start | bytes 589828
  376.5 106.7 %copy-start.81 = (s32[128]{0:T(128)S(1)}, s32[128]{0:T(128)}, u32[]{:S(2)}) copy-start(s32[128]{0:T(128)} %param.20) | copy-start | bytes 1540
  376.5 108.5 %copy-start.91 = (s32[256]{0:T(256)S(1)}, s32[256]{0:T(256)}, u32[]{:S(2)}) copy-start(s32[256]{0:T(256)} %param.21) | copy-start | bytes 3076
  376.6 1103.6 %reduce-scatter.45.cloned.1.call-start = ((), (), s32[]{:S(2)}) async-start(), calls=%async_computation.37 | async-start | bytes 1474560 | tf_op jit(solution)/shard_map/reduce_scatter | solution.py:290
  1423.2 58.9 %reduce-scatter.47.cloned.1.call-start = ((), (), s32[]{:S(2)}) async-start(), calls=%async_computation.38 | async-start | bytes 1474560 | tf_op jit(solution)/shard_map/reduce_scatter | solution.py:293
  1427.7 77.4 %reduce-scatter.49.cloned.1.call-start = ((), (), s32[]{:S(2)}) async-start(), calls=%async_computation.39 | async-start | bytes 1474560 | tf_op jit(solution)/shard_map/reduce_scatter | solution.py:296
  1432.4 100.7 %reduce-scatter.51.cloned.1.call-start = ((), (), s32[]{:S(2)}) async-start(), calls=%async_computation.40 | async-start | bytes 1474560 | tf_op jit(solution)/shard_map/reduce_scatter | solution.py:299
  1434.1 127.0 %reduce-scatter.53.cloned.1.call-start = ((), (), s32[]{:S(2)}) async-start(), calls=%async_computation.41 | async-start | bytes 1474560 | tf_op jit(solution)/shard_map/reduce_scatter | solution.py:302
  1436.7 152.6 %reduce-scatter.55.cloned.1.call-start = ((), (), s32[]{:S(2)}) async-start(), calls=%async_computation.42 | async-start | bytes 1474560 | tf_op jit(solution)/shard_map/reduce_scatter | solution.py:305
  1439.5 177.9 %reduce-scatter.57.cloned.1.call-start = ((), (), s32[]{:S(2)}) async-start(), calls=%async_computation.43 | async-start | bytes 1474560 | tf_op jit(solution)/shard_map/reduce_scatter | solution.py:308
  1441.6 204.0 %reduce-scatter.59.cloned.1.call-start = ((), (), s32[]{:S(2)}) async-start(), calls=%async_computation.44 | async-start | bytes 1474560 | tf_op jit(solution)/shard_map/reduce_scatter | solution.py:311
  1443.3 243.1 %reduce-scatter.61.cloned.1.call-start = ((), (), s32[]{:S(2)}) async-start(), calls=%async_computation.45 | async-start | bytes 3932160 | tf_op jit(solution)/shard_map/reduce_scatter | solution.py:314
  1446.0 280.6 %reduce-scatter.65.cloned.1.call-start = ((), (), s32[]{:S(2)}) async-start(), calls=%async_computation.47 | async-start | bytes 3932160 | tf_op jit(solution)/shard_map/reduce_scatter | solution.py:317
  1449.7 317.2 %reduce-scatter.69.cloned.1.call-start = ((), (), s32[]{:S(2)}) async-start(), calls=%async_computation.49 | async-start | bytes 3932160 | tf_op jit(solution)/shard_map/reduce_scatter | solution.py:320
  1453.7 1088.7 %reduce-scatter.91.cloned.1.call-start = ((), (), s32[]{:S(2)}) async-start(), calls=%async_computation.60 | async-start | bytes 55517184
  1480.1 1126.8 %reduce-scatter.73.cloned.1.call-start = ((), (), s32[]{:S(2)}) async-start(), calls=%async_computation.51 | async-start | bytes 442368
  1482.1 1189.3 %reduce-scatter.75.cloned.1.call-start = ((), (), s32[]{:S(2)}) async-start(), calls=%async_computation.52 | async-start | bytes 442368
  1484.0 1251.7 %reduce-scatter.77.cloned.1.call-start = ((), (), s32[]{:S(2)}) async-start(), calls=%async_computation.53 | async-start | bytes 442368
  1507.0 1293.2 %reduce-scatter.79.cloned.1.call-start = ((), (), s32[]{:S(2)}) async-start(), calls=%async_computation.54 | async-start | bytes 442368
  1535.0 1329.5 %reduce-scatter.81.cloned.1.call-start = ((), (), s32[]{:S(2)}) async-start(), calls=%async_computation.55 | async-start | bytes 442368
  1563.0 1365.9 %reduce-scatter.83.cloned.1.call-start = ((), (), s32[]{:S(2)}) async-start(), calls=%async_computation.56 | async-start | bytes 442368
  1591.2 1402.3 %reduce-scatter.85.cloned.1.call-start = ((), (), s32[]{:S(2)}) async-start(), calls=%async_computation.57 | async-start | bytes 442368
  1619.3 1438.6 %reduce-scatter.87.cloned.1.call-start = ((), (), s32[]{:S(2)}) async-start(), calls=%async_computation.58 | async-start | bytes 442368
  1647.4 1476.0 %reduce-scatter.63.cloned.1.call-start = ((), (), s32[]{:S(2)}) async-start(), calls=%async_computation.46 | async-start | bytes 884736 | tf_op jit(solution)/shard_map/reduce_scatter | solution.py:349
  1686.4 1502.7 %reduce-scatter.67.cloned.1.call-start = ((), (), s32[]{:S(2)}) async-start(), calls=%async_computation.48 | async-start | bytes 884736 | tf_op jit(solution)/shard_map/reduce_scatter | solution.py:352
  1726.7 1528.6 %reduce-scatter.71.cloned.1.call-start = ((), (), s32[]{:S(2)}) async-start(), calls=%async_computation.50 | async-start | bytes 884736 | tf_op jit(solution)/shard_map/reduce_scatter | solution.py:355
  1767.0 1548.6 %reduce-scatter.89.cloned.1.call-start = ((), (), s32[]{:S(2)}) async-start(), calls=%async_computation.59 | async-start | bytes 7864320
  (90 other events, 619.6 us)
Sparse Core Ops, SparseCore 0:
  9.6 49.0 all-gather.35
  60.8 17.4 all-gather.13
  80.5 17.4 all-gather.15
  105.8 18.5 all-gather.17
  137.7 18.5 all-gather.21
  170.0 18.3 all-gather.19
  201.9 18.5 all-gather.23
  234.0 18.7 all-gather.25
  266.2 18.8 all-gather.27
  300.5 29.6 all-gather.29
  334.2 30.0 all-gather.31
  367.9 30.7 all-gather.33
  400.2 934.4 all-gather.37
  1423.4 25.5 reduce-scatter.44
  1451.4 25.5 reduce-scatter.46
  1479.4 25.5 reduce-scatter.48
  1507.5 25.5 reduce-scatter.50
  1535.5 25.5 reduce-scatter.52
  1563.7 25.5 reduce-scatter.54
  1591.7 25.5 reduce-scatter.56
  1619.9 25.5 reduce-scatter.58
  1648.6 37.6 reduce-scatter.60
  1688.9 37.7 reduce-scatter.64
  1729.1 37.8 reduce-scatter.68
  1770.9 771.3 reduce-scatter.90
  2545.5 61.3 reduce-scatter.72
  2610.0 61.2 reduce-scatter.74
  2674.6 61.1 reduce-scatter.76
  2739.0 61.1 reduce-scatter.78
  2803.3 61.1 reduce-scatter.80
  2867.8 61.1 reduce-scatter.82
  2932.3 61.1 reduce-scatter.84
  2996.6 61.1 reduce-scatter.86
  3061.1 62.2 reduce-scatter.62
  3126.8 62.2 reduce-scatter.66
  3192.3 62.9 reduce-scatter.70
  3257.7 57.8 reduce-scatter.88
where the time goes:
time: 3340 us; the launch traced here: 3330 us
  waiting for transfers between devices  2560 us (77%)
  blocking collectives  497 us (15%)
  matrix products  151 us (5%)
  local copies, waits for them, and re-layouts  79 us (2%)
    unnamed x47, waiting for transfers between devices  1280 us
    all_gather x1, waiting for transfers between devices, body(): lax.all_gather(table_local, 'fsdp', axis=0, tiled=True)  814 us
    unnamed x1, blocking collectives  106 us
  transfers between devices with their start and end apart: 37, of which 23 were waited for; matrix products, arithmetic and copies ran while one was open for 4% of the time, Pallas kernels for 0%

commit v1 on v0

v1 whole, which is shorter than its diff:
```python
import jax
import jax.numpy as jnp
from jax import lax
from jax.sharding import PartitionSpec as P

D = 768
HEADS = 12
HEAD_DIM = 64


EPS = 1e-06
NEG = -1e30


def normalize(values):
    return values * lax.rsqrt(jnp.mean(values * values, axis=-1, keepdims=True) + EPS)


def norm_back(values, gain, grad, factor):

    def scaled(inner, weight):
        return normalize(inner) * weight * factor

    _, pull = jax.vjp(scaled, values, gain)
    return pull(grad)


def matmul(left, right):
    return jnp.dot(left, right, preferred_element_type=jnp.float32)


def times_transposed(left, right):
    return lax.dot_general(
        left, right, (((1,), (1,)), ((), ())), preferred_element_type=jnp.float32
    )


def transposed_times(left, right):
    return lax.dot_general(
        left, right, (((0,), (0,)), ((), ())), preferred_element_type=jnp.float32
    )


def split_heads(values):
    return values.reshape(values.shape[0], HEADS, HEAD_DIM)


def join_heads(values):
    return values.reshape(values.shape[0], HEADS * HEAD_DIM)


def masked_scores(query, keys, mask):
    scores = jnp.einsum(
        "thd,shd->hts", split_heads(query), split_heads(keys), preferred_element_type=jnp.float32
    )
    return jnp.where(mask[None], scores, NEG)


def attend(query, keys, values, mask):
    scores = masked_scores(query, keys, mask)
    top = jnp.max(scores, axis=-1, keepdims=True)
    normalizer = top + jnp.log(jnp.sum(jnp.exp(scores - top), axis=-1, keepdims=True))
    shares = jnp.exp(scores - normalizer).astype(jnp.bfloat16)
    mixed = jnp.einsum(
        "hts,shd->thd", shares, split_heads(values), preferred_element_type=jnp.float32
    )
    return (join_heads(mixed).astype(jnp.bfloat16), normalizer)


def attend_back(query, keys, values, mask, normalizer, out_grad):
    shares = jnp.exp(masked_scores(query, keys, mask) - normalizer)
    heads_grad = split_heads(out_grad)
    share_grad = jnp.einsum(
        "thd,shd->hts", heads_grad, split_heads(values), preferred_element_type=jnp.float32
    )
    inner = jnp.sum(shares * share_grad, axis=-1, keepdims=True)
    score_grad = (shares * (share_grad - inner)).astype(jnp.bfloat16)
    query_grad = jnp.einsum(
        "hts,shd->thd", score_grad, split_heads(keys), preferred_element_type=jnp.float32
    )
    key_grad = jnp.einsum(
        "hts,thd->shd", score_grad, split_heads(query), preferred_element_type=jnp.float32
    )
    value_grad = jnp.einsum(
        "hts,thd->shd", shares.astype(jnp.bfloat16), heads_grad, preferred_element_type=jnp.float32
    )
    return (
        join_heads(query_grad).astype(jnp.bfloat16),
        join_heads(key_grad).astype(jnp.bfloat16),
        join_heads(value_grad).astype(jnp.bfloat16),
    )


def swap(value, axis, step):
    size = lax.axis_size(axis)
    return lax.ppermute(value, axis, [(place, place ^ step) for place in range(size)])


def relative_order(size):
    order, step = [0], size // 2
    while step:
        order = order + [place | step for place in order]
        step //= 2
    return order


def gather_relative(value, axis):
    stack, step = value[None], lax.axis_size(axis) // 2
    while step:
        stack = jnp.concatenate([stack, swap(stack, axis, step)], axis=0)
        step //= 2
    return stack


def exchange_relative(blocks, axis):
    me = lax.axis_index(axis)
    got = []
    for step in relative_order(lax.axis_size(axis)):
        block = lax.dynamic_index_in_dim(blocks, me ^ step, 0, keepdims=False)
        got.append(block if step == 0 else swap(block, axis, step))
    return jnp.stack(got)


def column_blocks(values, count):
    rows, width = values.shape
    return values.reshape(rows, count, width // count).transpose(1, 0, 2)


def flat_rows(stack):
    return stack.reshape(stack.shape[0] * stack.shape[1], stack.shape[2])


def body(
    hidden,
    memory,
    tgt_segments,
    mem_segments,
    labels,
    self_query,
    self_key,
    self_value,
    self_out,
    cross_query,
    cross_key,
    cross_value,
    cross_out,
    gate_weight,
    up_weight,
    down_weight,
    norm_gains,
    embedding,
):
    wide, deep = lax.axis_size("dp"), lax.axis_size("fsdp")
    rows, cols = self_query.shape
    ff_cols, ff_rows = gate_weight.shape[1], down_weight.shape[0]
    ff = ff_cols * wide
    folds = cols // rows
    gain_column = jnp.zeros((rows, 128), jnp.bfloat16).at[: norm_gains.shape[0], 0].set(norm_gains)
    down_turned = down_weight.T.reshape(folds, rows, ff_rows).transpose(1, 0, 2)
    pack = jnp.concatenate(
        [
            self_query,
            self_key,
            self_value,
            self_out,
            cross_query,
            cross_key,
            cross_value,
            cross_out,
            gate_weight,
            up_weight,
            down_turned.reshape(rows, folds * ff_rows),
            gain_column,
        ],
        axis=1,
    )
    gathered = lax.all_gather(pack, ("dp", "fsdp"), axis=0, tiled=True)
    gathered = gathered.reshape(wide, deep * rows, pack.shape[1])
    table = lax.all_gather(embedding, "dp", axis=1, tiled=True)

    def columns_of(start, width):
        return gathered[:, :, start : start + width].transpose(1, 0, 2).reshape(D, wide * width)

    squares = [columns_of(index * cols, cols) for index in range(8)]
    query_full, key_full, value_full, output_full = squares[:4]
    recall_query, recall_key, recall_value, recall_output = squares[4:]
    at = 8 * cols
    gate_full = columns_of(at, ff_cols)
    up_full = columns_of(at + ff_cols, ff_cols)
    at = at + 2 * ff_cols
    down_turned = (
        gathered[:, :, at : at + folds * ff_rows]
        .reshape(wide, deep, rows, folds, ff_rows)
        .transpose(0, 3, 2, 1, 4)
        .reshape(D, ff)
    )
    at = at + folds * ff_rows
    gains = gathered[:, :, at].reshape(wide, deep, rows)[:, :, : norm_gains.shape[0]]
    gains = gains.astype(jnp.float32).reshape(4, D)

    inputs = hidden.astype(jnp.float32)
    length = hidden.shape[0]
    places = jnp.arange(length)
    self_mask = (tgt_segments[:, None] == tgt_segments[None, :]) & (
        places[None, :] <= places[:, None]
    )
    cross_mask = (tgt_segments[:, None] == mem_segments[None, :]) | (tgt_segments[:, None] == 0)
    valid = (tgt_segments > 0).astype(jnp.int32)
    group_marks = lax.all_gather(jnp.stack([labels, valid]), "fsdp", axis=1, tiled=True)
    group_labels, group_valid = group_marks[0], group_marks[1].astype(jnp.float32)
    memory_near = flat_rows(gather_relative(memory, "dp"))

    first_normed = (normalize(inputs) * gains[0]).astype(jnp.bfloat16)
    queries = matmul(first_normed, query_full).astype(jnp.bfloat16)
    keys = matmul(first_normed, key_full).astype(jnp.bfloat16)
    values = matmul(first_normed, value_full).astype(jnp.bfloat16)
    attended, self_norms = attend(queries, keys, values, self_mask)
    after_self = inputs + matmul(attended, output_full)
    second_normed = (normalize(after_self) * gains[1]).astype(jnp.bfloat16)
    asked = matmul(second_normed, recall_query).astype(jnp.bfloat16)
    memory_keys = matmul(memory, recall_key).astype(jnp.bfloat16)
    memory_values = matmul(memory, recall_value).astype(jnp.bfloat16)
    recalled, cross_norms = attend(asked, memory_keys, memory_values, cross_mask)
    after_cross = after_self + matmul(recalled, recall_output)
    third_normed = (normalize(after_cross) * gains[2]).astype(jnp.bfloat16)
    gate_rows = matmul(third_normed, gate_full)
    up_rows = matmul(third_normed, up_full)
    activated = (jax.nn.gelu(gate_rows, approximate=True) * up_rows).astype(jnp.bfloat16)
    block_sum = after_cross + times_transposed(activated, down_turned)
    exit_rows = (normalize(block_sum) * gains[3] * D ** (-0.5)).astype(jnp.bfloat16)

    group_exit = lax.all_gather(exit_rows, "fsdp", axis=0, tiled=True)
    factors = jnp.concatenate(
        [first_normed, attended, second_normed, recalled, third_normed, activated], axis=1
    )
    near = flat_rows(gather_relative(factors, "dp"))
    first_near = near[:, :D]
    attended_near = near[:, D : 2 * D]
    second_near = near[:, 2 * D : 3 * D]
    recalled_near = near[:, 3 * D : 4 * D]
    third_near = near[:, 4 * D : 5 * D]
    activated_near = near[:, 5 * D :]

    logits = times_transposed(group_exit, table)
    vocab = table.shape[0]
    first_entry = lax.axis_index("fsdp") * vocab
    onehot = (
        jnp.arange(vocab)[None, :] == (group_labels - first_entry)[:, None]
    ).astype(jnp.float32)
    top = jnp.max(logits, axis=1)
    raised = jnp.sum(jnp.exp(logits - top[:, None]), axis=1)
    picked = jnp.sum(onehot * logits, axis=1)
    stats = lax.all_gather(jnp.stack([top, raised, picked]), "fsdp", axis=0, tiled=False)
    top = jnp.max(stats[:, 0], axis=0)
    normalizer = top + jnp.log(jnp.sum(stats[:, 1] * jnp.exp(stats[:, 0] - top), axis=0))
    group_loss = jnp.sum((normalizer - jnp.sum(stats[:, 2], axis=0)) * group_valid)
    logit_grad = (
        (jnp.exp(logits - normalizer[:, None]) - onehot) * group_valid[:, None]
    ).astype(jnp.bfloat16)
    exit_grad = lax.psum_scatter(
        matmul(logit_grad, table).astype(jnp.bfloat16), "fsdp", scatter_dimension=0, tiled=True
    ).astype(jnp.float32)
    grad_embedding = lax.psum_scatter(
        transposed_times(logit_grad, group_exit).astype(jnp.bfloat16),
        "dp",
        scatter_dimension=1,
        tiled=True,
    ).astype(jnp.float32)

    block_grad, exit_gain = norm_back(block_sum, gains[3], exit_grad, D ** (-0.5))
    down_input = block_grad.astype(jnp.bfloat16)
    act_grad = matmul(down_input, down_turned)
    _, pull = jax.vjp(
        lambda gate_in, up_in: jax.nn.gelu(gate_in, approximate=True) * up_in, gate_rows, up_rows
    )
    gate_grad, up_grad = pull(act_grad)
    gate_grad = gate_grad.astype(jnp.bfloat16)
    up_grad = up_grad.astype(jnp.bfloat16)

    def share(*grads):
        blocks = jnp.concatenate([column_blocks(grad, wide) for grad in grads], axis=2)
        got = flat_rows(exchange_relative(blocks, "dp"))
        parts, at = [], 0
        for grad in grads:
            width = grad.shape[1] // wide
            parts.append(got[:, at : at + width])
            at += width
        return parts

    gate_near, up_near, down_near = share(gate_grad, up_grad, down_input)
    grad_gate = transposed_times(third_near, gate_near)
    grad_up = transposed_times(third_near, up_near)
    grad_down = transposed_times(down_near, activated_near)
    grad_down = (
        grad_down.reshape(folds, rows, deep, ff_rows)
        .transpose(2, 1, 0, 3)
        .reshape(D, folds * ff_rows)
    )
    ff_grads = lax.psum_scatter(
        jnp.concatenate([grad_gate, grad_up, grad_down], axis=1).astype(jnp.bfloat16),
        "fsdp",
        scatter_dimension=0,
        tiled=True,
    )

    third_grad = times_transposed(gate_grad, gate_full) + times_transposed(up_grad, up_full)
    cross_back, third_gain = norm_back(after_cross, gains[2], third_grad, 1.0)
    after_cross_grad = block_grad + cross_back
    cross_branch = after_cross_grad.astype(jnp.bfloat16)
    recalled_grad = times_transposed(cross_branch, recall_output).astype(jnp.bfloat16)
    probe_grad, lookup_grad, content_grad = attend_back(
        asked, memory_keys, memory_values, cross_mask, cross_norms, recalled_grad
    )
    grad_memory = times_transposed(lookup_grad, recall_key) + times_transposed(
        content_grad, recall_value
    )
    second_grad = times_transposed(probe_grad, recall_query)
    self_back, second_gain = norm_back(after_self, gains[1], second_grad, 1.0)
    after_self_grad = after_cross_grad + self_back
    self_branch = after_self_grad.astype(jnp.bfloat16)
    cross_near, probe_near = share(cross_branch, probe_grad)
    lookup_near, content_near = share(lookup_grad, content_grad)
    attended_grad = times_transposed(self_branch, output_full).astype(jnp.bfloat16)
    query_grad, key_grad, value_grad = attend_back(
        queries, keys, values, self_mask, self_norms, attended_grad
    )
    self_near, query_near, key_near, value_near = share(
        self_branch, query_grad, key_grad, value_grad
    )
    square_grads = lax.psum_scatter(
        jnp.concatenate(
            [
                transposed_times(first_near, query_near),
                transposed_times(first_near, key_near),
                transposed_times(first_near, value_near),
                transposed_times(attended_near, self_near),
                transposed_times(second_near, probe_near),
                transposed_times(memory_near, lookup_near),
                transposed_times(memory_near, content_near),
                transposed_times(recalled_near, cross_near),
            ],
            axis=1,
        ).astype(jnp.bfloat16),
        "fsdp",
        scatter_dimension=0,
        tiled=True,
    )
    first_grad = (
        times_transposed(query_grad, query_full)
        + times_transposed(key_grad, key_full)
        + times_transposed(value_grad, value_full)
    )
    input_back, first_gain = norm_back(inputs, gains[0], first_grad, 1.0)
    grad_hidden = after_self_grad + input_back

    owned = [
        square_grads[:, index * cols : (index + 1) * cols].astype(jnp.float32)
        for index in range(8)
    ]
    owned.append(ff_grads[:, :ff_cols].astype(jnp.float32))
    owned.append(ff_grads[:, ff_cols : 2 * ff_cols].astype(jnp.float32))
    owned.append(
        ff_grads[:, 2 * ff_cols :]
        .reshape(rows, folds, ff_rows)
        .transpose(1, 0, 2)
        .reshape(cols, ff_rows)
        .T.astype(jnp.float32)
    )
    gain_grad = lax.psum_scatter(
        jnp.concatenate([first_gain, second_gain, third_gain, exit_gain]),
        ("dp", "fsdp"),
        scatter_dimension=0,
        tiled=True,
    )
    loss_total = lax.psum(group_loss, "dp")
    loss_mean = loss_total / (length * wide * deep)
    return (
        block_sum.astype(jnp.bfloat16),
        loss_mean,
        grad_hidden,
        grad_memory,
        *owned,
        gain_grad,
        grad_embedding,
    )


def solution(mesh):
    in_specs = (
        P(("dp", "fsdp"), None),
        P(("dp", "fsdp"), None),
        P(("dp", "fsdp")),
        P(("dp", "fsdp")),
        P(("dp", "fsdp")),
        P("fsdp", "dp"),
        P("fsdp", "dp"),
        P("fsdp", "dp"),
        P("fsdp", "dp"),
        P("fsdp", "dp"),
        P("fsdp", "dp"),
        P("fsdp", "dp"),
        P("fsdp", "dp"),
        P("fsdp", "dp"),
        P("fsdp", "dp"),
        P("fsdp", "dp"),
        P(("dp", "fsdp")),
        P("fsdp", "dp"),
    )
    out_specs = (
        P(("dp", "fsdp"), None),
        P(),
        P(("dp", "fsdp"), None),
        P(("dp", "fsdp"), None),
        P("fsdp", "dp"),
        P("fsdp", "dp"),
        P("fsdp", "dp"),
        P("fsdp", "dp"),
        P("fsdp", "dp"),
        P("fsdp", "dp"),
        P("fsdp", "dp"),
        P("fsdp", "dp"),
        P("fsdp", "dp"),
        P("fsdp", "dp"),
        P("fsdp", "dp"),
        P(("dp", "fsdp")),
        P("fsdp", "dp"),
    )
    return jax.shard_map(body, mesh=mesh, in_specs=in_specs, out_specs=out_specs, check_vma=False)
```

time: 3340 us -> 680 us (0.20)
  waiting for transfers between devices: 2560 us -> 303 us
  blocking collectives: 497 us -> 94.6 us
  matrix products: 151 us -> 87.5 us
    unnamed x47 -> x9, waiting for transfers between devices: 1280 us -> 35.9 us
    all_gather x13 -> x3, waiting for transfers between devices: 814 us -> 131 us  [the longest x1 128 us: body(): gathered = lax.all_gather(pack, ('dp', 'fsdp'), axis=0, tiled=True)]
    reduce_scatter x14 -> x2, waiting for transfers between devices: 463 us -> 90.8 us  [the longest x1 56.9 us: body(): lax.psum_scatter(transposed_times(logit_grad, group_exit).astype(jnp.bflo...]
    all_gather x11 -> x2, blocking collectives: 352 us -> 48 us  [the longest x1 30.5 us: body(): lax.all_gather(jnp.stack([top, raised, picked]), 'fsdp', axis=0, tiled=Fa...]
    unnamed x1, blocking collectives: 106 us -> 39.1 us
    ppermute x0 -> x16, waiting for transfers between devices: none -> 44.8 us  [swap(): lax.ppermute(value, axis, [(place, place ^ step) for place in range(size)])]
    transpose x0 -> x12, local copies, waits for them, and re-layouts: none -> 38.4 us  [the longest x11 34.7 us: columns_of(): gathered[:, :, start:start + width].transpose(1, 0, 2)]
  transfers between devices with their start and end apart: 37 -> 23, of which waited for: 23 -> 11; matrix products, arithmetic and copies ran while one was open for 4% -> 29% of each run, Pallas kernels for 0% -> 0%
where the time goes in v1:
time: 680 us; the launch traced here: 670 us
  waiting for transfers between devices  303 us (45%)
  local copies, waits for them, and re-layouts  105 us (15%)
  blocking collectives  94.6 us (14%)
  matrix products  87.5 us (13%)
  other arithmetic  51.1 us (8%)
  between operations  18.1 us (3%)
  starting transfers between devices  11.2 us (2%)
    all_gather x1, waiting for transfers between devices, body(): gathered = lax.all_gather(pack, ('dp', 'fsdp'), axis=0, tiled=True)  128 us
    reduce_scatter x1, waiting for transfers between devices, body(): lax.psum_scatter(transposed_times(logit_grad, group_exit).astype(jnp.bflo...  56.9 us
    ppermute x16, waiting for transfers between devices, swap(): lax.ppermute(value, axis, [(place, place ^ step) for place in range(size)])  44.8 us
    unnamed x1, blocking collectives  39.1 us
    unnamed x9, waiting for transfers between devices  35.9 us
    transpose x11, local copies, waits for them, and re-layouts, columns_of(): gathered[:, :, start:start + width].transpose(1, 0, 2)  34.7 us
    reduce_scatter x1, waiting for transfers between devices, body(): lax.psum_scatter(matmul(logit_grad, table).astype(jnp.bfloat16), 'fsdp',...  33.9 us
    all_gather x1, blocking collectives, body(): lax.all_gather(jnp.stack([top, raised, picked]), 'fsdp', axis=0, tiled=Fa...  30.5 us
  transfers between devices with their start and end apart: 23, of which 11 were waited for; matrix products, arithmetic and copies ran while one was open for 29% of the time, Pallas kernels for 0%

profile of v1, /device:TPU:0, one launch (start us, length us, event | category | flops | bytes accessed | tf_op | source)
XLA Modules:
  0.0 669.6 jit_solution(2434695774449361896)
XLA Ops:
  10.4 2.0 concatenate.45
  14.7 128.2 %all-gather.6.cloned.1.call-done = bf16[3072,3200]{1,0:T(8,128)(2,1)} async-done(((bf16[96,3200]{1,0:T(8,128)(2,1)}), bf16[3072,3200]{1,0:T(8,128)(2,1)}) %all-gather.6.cloned.1.call-update) | async-done | bytes 19660816 | tf_op jit(solution)/shard_map/all_gather | solution.py:177
  142.9 10.2 %slice_bitcast_fusion.2 = (bf16[768,4,192]{2,0,1:T(8,128)(2,1)}, bf16[768,4,192]{2,0,1:T(8,128)(2,1)}, bf16[768,4,192]{2,0,1:T(8,128)(2,1)}, bf16[768,4,192]{2,0...) fusion(bf16[4,768,3200]{2,1,0:T(8,128)(2,1)} %bitcast.262), kind=kLoop, calls=%fused_computation.13 | loop fusion | bytes 18874368 | tf_op jit(solution)/shard_map/transpose | solution.py:182
  153.1 1.9 copy.186
  159.8 1.8 copy.190
  162.3 2.6 copy.193
  164.9 2.6 copy.194
  171.2 1.9 convolution_convert_fusion.24
  173.3 2.7 copy.197
  177.5 1.8 convolution_convert_fusion.7
  182.6 7.0 %fusion.85 = (bf16[4,768,512]{2,1,0:T(8,128)(2,1)}, bf16[768,4,512]{2,0,1:T(8,128)(2,1)}, bf16[768,4,512]{2,0,1:T(8,128)(2,1)}) fusion(bf16[4,768,3200]{2,1,0:T(8,128)(2,1)} %bitcast.264), kind=kLoop, calls=%fused_computation.235 | loop fusion | bytes 18874368 | tf_op jit(solution)/shard_map/slice | solution.py:192
  189.6 4.7 copy.199
  194.4 4.7 copy.200
  199.0 5.7 reshape.457
  204.7 3.7 copy.201
  210.0 1.8 copy-done.15
  214.9 2.2 constant_dynamic-update-slice_fusion
  220.7 17.5 %all_gather.21 = s32[2,1024]{1,0:T(2,128)S(1)} all-gather(s32[2,128]{1,0:T(2,128)S(1)} %pad_add_fusion), channel_id=1, replica_groups=mesh['dp'=4,'fsdp'=8] {'fsdp'}, dimensions={1}, use_global_device_ids=true | all-gather | bytes 9216 | tf_op jit(solution)/shard_map/all_gather | solution.py:209
  238.3 16.4 %collective-permute-done = bf16[1,128,5888]{2,1,0:T(8,128)(2,1)} collective-permute-done((bf16[1,128,5888]{2,1,0:T(8,128)(2,1)}, bf16[1,128,5888]{2,1,0:T(8,128)(2,1)}, u32[]{:S(2)}, u32[]{:S(2)}) %collective-permute-start) | collective-permute-done | bytes 1507360 | tf_op jit(solution)/shard_map/ppermute | solution.py:96
  254.7 3.7 pad_maximum_fusion.1
  258.4 2.9 all-gather.8.cloned.1.call-done
  261.3 13.1 %fusion.91 = (f32[1024]{0:T(1024)S(1)}, f32[1024,4016]{0,1:T(8,128)}) fusion(bf16[1024,768]{1,0:T(8,128)(2,1)} %all-gather.8.cloned.1.call-done, bf16[4016,768]{0,1:T(8,128)(2,1)} %all-gather.10.cloned.1.call-done), kind=kOutput, calls=%fused_computation.241 | convolution fusion | flops 6320733184 | bytes 24195072 | tf_op jit(solution)/shard_map/dot_general | solution.py:33
  274.4 8.3 %exponential_reduce_fusion = (f32[1024]{0:T(1024)S(1)}, f32[1024]{0:T(1024)S(1)}) fusion(f32[1024,4016]{0,1:T(8,128)} %get-tuple-element.184, f32[1024]{0:T(1024)S(1)} %get-tuple-element.183, s32[1024]{0:T(1024)S(1)} %bitcast.371), kind=kLoop, calls=%fused_computation.3 | loop fusion | flops 20559872 | bytes 16465920 | tf_op jit(solution)/shard_map/reduce_sum | solution.py:251
  282.7 30.5 %all-gather.1 = f32[8,3,1024]{2,1,0:T(4,128)S(1)} all-gather(f32[1,3,1024]{2,1,0:T(4,128)S(1)} %maximum_bitcast_fusion), channel_id=2, replica_groups=mesh['dp'=4,'fsdp'=8] {'fsdp'}, dimensions={0}, use_global_device_ids=true | all-gather | bytes 110592 | tf_op jit(solution)/shard_map/all_gather | solution.py:253
  314.0 14.8 %convolution_convert_fusion.2 = bf16[1024,768]{1,0:T(8,128)(2,1)} fusion(bf16[4016,768]{0,1:T(8,128)(2,1)S(1)} %copy-done.104, f32[1024,4016]{0,1:T(8,128)} %get-tuple-element.184, f32[1024]{0:T(1024)S(1)} %bitcast.375, f32[1024]{0:T(1024)S(1)} %get-tuple-element.122, s32[1024]{0:T(1024)S(1)} %bitcast.372), kind=kOutput, calls=%fused_computation.12 | convolution fusion | flops 6342082560 | bytes 24203264 | tf_op jit(solution)/shard_map/dot_general | solution.py:29
  330.4 6.5 collective-permute-done.8
  337.6 1.9 pad_maximum_fusion.8
  339.6 2.6 collective-permute-done.9
  342.2 2.7 pad_maximum_fusion.3
  344.9 14.1 %pad_maximum_fusion = bf16[4,128,5888]{2,1,0:T(8,128)(2,1)} fusion(bf16[2,128,5888]{2,1,0:T(8,128)(2,1)} %collective-permute-done.1, bf16[1,128,5888]{2,1,0:T(8,128)(2,1)} %collective-permute-done, bf16[1,128,5888]{2,1,0:T(8,128)(2,1)S(1)} %bitcast.283), kind=kLoop, calls=%fused_computation.5 | loop fusion | flops 6029312 | bytes 12058624 | tf_op jit(solution)/shard_map/concatenate | solution.py:110
  359.0 33.9 %reduce-scatter.9.cloned.1.call-done = bf16[128,768]{1,0:T(8,128)(2,1)} async-done(((bf16[1024,768]{1,0:T(8,128)(2,1)}), bf16[128,768]{1,0:T(8,128)(2,1)}) %reduce-scatter.9.cloned.1.call-update) | async-done | bytes 196624 | tf_op jit(solution)/shard_map/reduce_scatter | solution.py:260
  395.7 4.0 multiply_convert_fusion.2
  430.7 5.0 collective-permute-done.5
  441.0 1.8 fusion.8
  446.0 1.8 fusion.5
  453.6 2.4 copy.251
  460.2 7.1 %collective-permute-done.15 = bf16[128,1216]{0,1:T(8,128)(2,1)S(1)} collective-permute-done((bf16[128,1216]{0,1:T(8,128)(2,1)S(1)}, bf16[128,1216]{0,1:T(8,128)(2,1)S(1)}, u32[]{:S(2)}, u32[]{:S(2)}) %collective-permute-start.15) | collective-permute-done | bytes 311328 | tf_op jit(solution)/shard_map/ppermute | solution.py:96
  467.3 7.1 %collective-permute-done.13 = bf16[128,1216]{0,1:T(8,128)(2,1)S(1)} collective-permute-done((bf16[128,1216]{0,1:T(8,128)(2,1)S(1)}, bf16[128,1216]{0,1:T(8,128)(2,1)S(1)}, u32[]{:S(2)}, u32[]{:S(2)}) %collective-permute-start.13) | collective-permute-done | bytes 311328 | tf_op jit(solution)/shard_map/ppermute | solution.py:96
  476.0 2.4 convolution_convert_fusion.1
  480.7 1.8 convolution_convert_fusion.3
  482.5 1.8 convolution_convert_fusion.4
  484.5 2.5 copy.253
  488.5 12.8 %convolution_convert_fusion = bf16[4016,768]{0,1:T(8,128)(2,1)} fusion(bf16[1024,768]{1,0:T(8,128)(2,1)S(1)} %copy-done.105, f32[1024,4016]{0,1:T(8,128)} %get-tuple-element.184, f32[1024]{0:T(1024)S(1)} %bitcast.376, f32[1024]{0:T(1024)S(1)} %copy-done.96, s32[1024]{0:T(1024)S(1)} %bitcast.373), kind=kOutput, calls=%fused_computation.4 | convolution fusion | flops 6344380416 | bytes 24203264 | tf_op jit(solution)/shard_map/dot_general | solution.py:39
  501.3 7.4 %psum.7 = f32[]{:T(128)} all-reduce(f32[]{:T(128)} %get-tuple-element.121), channel_id=1, replica_groups=mesh['dp'=4,'fsdp'=8] {'dp'}, use_global_device_ids=true, to_apply=%region_16.17 | all-reduce | flops 1 | bytes 8 | tf_op jit(solution)/shard_map/psum | solution.py:375
  511.2 39.1 %all-reduce.1 = f32[3072]{0:T(1024)S(1)} all-reduce(f32[3072]{0:T(1024)S(1)} %pad_maximum_fusion.11), channel_id=6, replica_groups=mesh['dp'=4,'fsdp'=8] {'dp','fsdp'}, use_global_device_ids=true, to_apply=%region_30.31.clone | all-reduce | flops 3072 | bytes 24576
  562.0 35.1 %reduce-scatter.15.cloned.1.call-done = bf16[96,1536]{1,0:T(8,128)(2,1)} async-done(((bf16[768,1536]{1,0:T(8,128)(2,1)}), bf16[96,1536]{1,0:T(8,128)(2,1)}) %reduce-scatter.15.cloned.1.call-update) | async-done | bytes 294928
  600.9 56.9 %reduce-scatter.11.cloned.1.call-done = bf16[4016,192]{0,1:T(8,128)(2,1)} async-done(((bf16[4016,768]{0,1:T(8,128)(2,1)}), bf16[4016,192]{0,1:T(8,128)(2,1)}) %reduce-scatter.11.cloned.1.call-update) | async-done | bytes 1542160 | tf_op jit(solution)/shard_map/reduce_scatter | solution.py:263
  657.8 3.4 convert_element_type.345
  (409 shorter events, 104.9 us)
Async XLA Ops:
  7.2 135.7 %all-gather.6.cloned.1.call-start = ((), (), s32[]{:S(2)}) async-start(), calls=%async_computation.4 | async-start | bytes 20275200 | tf_op jit(solution)/shard_map/all_gather | solution.py:177
  12.4 246.0 %all-gather.10.cloned.1.call-start = ((), (), s32[]{:S(2)}) async-start(), calls=%async_computation.6 | async-start | bytes 7864320 | tf_op jit(solution)/shard_map/all_gather | solution.py:179
  13.2 248.1 %all-gather.8.cloned.1.call-start = ((), (), s32[]{:S(2)}) async-start(), calls=%async_computation.5 | async-start | bytes 1769472 | tf_op jit(solution)/shard_map/all_gather | solution.py:232
  13.3 139.7 %copy-start.98 = (f32[128]{0:T(128)}, f32[128]{0:T(128)S(1)}, u32[]{:S(2)}) copy-start(f32[128]{0:T(128)S(1)} %fusion.42) | copy-start | bytes 1540
  13.4 148.2 %copy-start.81 = (f32[128]{0:T(128)}, f32[128]{0:T(128)S(1)}, u32[]{:S(2)}) copy-start(f32[128]{0:T(128)S(1)} %fusion.73) | copy-start | bytes 1540
  157.6 3.9 copy-start.72
  157.6 13.6 %copy-start.76 = (f32[768]{0:T(1024)}, f32[768]{0:T(1024)S(1)}, u32[]{:S(2)}) copy-start(f32[768]{0:T(1024)S(1)} %get-tuple-element.101) | copy-start | bytes 9220
  158.3 11.1 %copy-start.50 = (bf16[128,768]{0,1:T(8,128)(2,1)}, bf16[128,768]{0,1:T(8,128)(2,1)S(1)}, u32[]{:S(2)}) copy-start(bf16[128,768]{0,1:T(8,128)(2,1)S(1)} %copy.187) | copy-start | bytes 589828
  159.8 9.2 %copy-start.41 = (bf16[128,768]{0,1:T(8,128)(2,1)}, bf16[128,768]{0,1:T(8,128)(2,1)S(1)}, u32[]{:S(2)}) copy-start(bf16[128,768]{0,1:T(8,128)(2,1)S(1)} %copy.189) | copy-start | bytes 589828
  162.3 6.7 copy-start.43
  173.3 6.0 copy-start.48
  209.6 7.5 %copy-start.4 = (bf16[96,8,8,256]{3,1,2,0:T(8,128)(2,1)}, bf16[96,8,8,256]{3,1,2,0:T(8,128)(2,1)S(1)}, u32[]{:S(2)}) copy-start(bf16[96,8,8,256]{3,1,2,0:T(8,128)(2,1)S(1)} %copy.271) | copy-start | bytes 9437188
  212.4 4.7 copy-start.17
  217.1 3.6 copy-start.102
  217.1 3.6 copy-start.103
  219.2 173.7 %reduce-scatter.9.cloned.1.call-start = ((), (), s32[]{:S(2)}) async-start(), calls=%async_computation.7 | async-start | bytes 1769472 | tf_op jit(solution)/shard_map/reduce_scatter | solution.py:260
  219.3 35.4 %collective-permute-start = (bf16[1,128,5888]{2,1,0:T(8,128)(2,1)}, bf16[1,128,5888]{2,1,0:T(8,128)(2,1)}, u32[]{:S(2)}, u32[]{:S(2)}) collective-permute-start(bf16[1,128,5888]{2,1,0:T(8,128)(2,1)} %bitcast.281), channel_id=1, source_target_pairs={{0,16},{8,24},{16,0},{24,8},{1,17},{9,25},{17,1},{25,9},{2,18},{10... | collective-permute-start | bytes 4521992 | tf_op jit(solution)/shard_map/ppermute | solution.py:96
  238.2 75.7 %copy-start.86 = (s32[1,1024]{1,0:T(1,128)}, s32[1,1024]{1,0:T(1,128)S(1)}, u32[]{:S(2)}) copy-start(s32[1,1024]{1,0:T(1,128)S(1)} %get-tuple-element.168) | copy-start | bytes 12292
  238.2 75.7 %copy-start.88 = (f32[1,1024]{1,0:T(1,128)}, f32[1,1024]{1,0:T(1,128)S(1)}, u32[]{:S(2)}) copy-start(f32[1,1024]{1,0:T(1,128)S(1)} %get-tuple-element.169) | copy-start | bytes 12292
  258.4 86.5 %collective-permute-start.1 = (bf16[2,128,5888]{2,1,0:T(8,128)(2,1)}, bf16[2,128,5888]{2,1,0:T(8,128)(2,1)}, u32[]{:S(2)}, u32[]{:S(2)}) collective-permute-start(bf16[2,128,5888]{2,1,0:T(8,128)(2,1)} %pad_maximum_fusion.1), channel_id=1, source_target_pairs={{0,8},{8,0},{16,24},{24,16},{1,9},{9,1},{17,25},{25,17},{2,10},{10... | collective-permute-start | bytes 9043976 | tf_op jit(solution)/shard_map/ppermute | solution.py:96
  274.4 39.6 %copy-start.104 = (bf16[4016,768]{0,1:T(8,128)(2,1)S(1)}, bf16[4016,768]{0,1:T(8,128)(2,1)}, u32[]{:S(2)}) copy-start(bf16[4016,768]{0,1:T(8,128)(2,1)} %all-gather.10.cloned.1.call-done) | copy-start | bytes 18505732
  314.0 14.8 %copy-start.95 = (f32[1024]{0:T(1024)}, f32[1024]{0:T(1024)S(1)}, u32[]{:S(2)}) copy-start(f32[1024]{0:T(1024)S(1)} %get-tuple-element.122) | copy-start | bytes 12292
  328.8 225.1 %reduce-scatter.13.cloned.1.call-start = ((), (), s32[]{:S(2)}) async-start(), calls=%async_computation.9 | async-start | bytes 2654208
  328.8 8.1 %collective-permute-start.8 = (bf16[1,256,768]{2,1,0:T(8,128)(2,1)}, bf16[1,256,768]{2,1,0:T(8,128)(2,1)S(1)}, u32[]{:S(2)}, u32[]{:S(2)}) collective-permute-start(bf16[1,256,768]{2,1,0:T(8,128)(2,1)} %bitcast.334), channel_id=1, source_target_pairs={{0,16},{8,24},{16,0},{24,8},{1,17},{9,25},{17,1},{25,9},{2,18},{10... | collective-permute-start | bytes 1179656 | tf_op jit(solution)/shard_map/ppermute | solution.py:96
  339.6 2.6 collective-permute-start.9
  339.6 5.3 copy-start.22
  395.7 4.0 copy-start.68
  395.7 4.0 copy-start.3
  417.9 8.4 %copy-start.29 = (bf16[12,64,256]{2,1,0:T(8,128)(2,1)}, bf16[12,64,256]{2,1,0:T(8,128)(2,1)S(1)}, u32[]{:S(2)}) copy-start(bf16[12,64,256]{2,1,0:T(8,128)(2,1)S(1)} %convolution_convert_fusion.5) | copy-start | bytes 1179652
  419.2 7.4 %collective-permute-start.7 = (bf16[128,384]{1,0:T(8,128)(2,1)}, bf16[128,384]{1,0:T(8,128)(2,1)}, u32[]{:S(2)}, u32[]{:S(2)}) collective-permute-start(bf16[128,384]{1,0:T(8,128)(2,1)} %bitcast.90), channel_id=1, source_target_pairs={{0,24},{8,16},{16,8},{24,0},{1,25},{9,17},{17,9},{25,1},{2,26},{10... | collective-permute-start | bytes 294920 | tf_op jit(solution)/shard_map/ppermute | solution.py:96
  420.2 16.6 %collective-permute-start.4 = (bf16[128,768]{1,0:T(8,128)(2,1)}, bf16[128,768]{1,0:T(8,128)(2,1)S(1)}, u32[]{:S(2)}, u32[]{:S(2)}) collective-permute-start(bf16[128,768]{1,0:T(8,128)(2,1)} %bitcast.79), channel_id=1, source_target_pairs={{0,24},{8,16},{16,8},{24,0},{1,25},{9,17},{17,9},{25,1},{2,26},{10... | collective-permute-start | bytes 589832 | tf_op jit(solution)/shard_map/ppermute | solution.py:96
  422.7 14.8 %collective-permute-start.3 = (bf16[128,768]{1,0:T(8,128)(2,1)}, bf16[128,768]{1,0:T(8,128)(2,1)}, u32[]{:S(2)}, u32[]{:S(2)}) collective-permute-start(bf16[128,768]{1,0:T(8,128)(2,1)} %bitcast.77), channel_id=1, source_target_pairs={{0,8},{8,0},{16,24},{24,16},{1,9},{9,1},{17,25},{25,17},{2,10},{10... | collective-permute-start | bytes 589832 | tf_op jit(solution)/shard_map/ppermute | solution.py:96
  423.6 15.0 %collective-permute-start.2 = (bf16[128,768]{1,0:T(8,128)(2,1)}, bf16[128,768]{1,0:T(8,128)(2,1)}, u32[]{:S(2)}, u32[]{:S(2)}) collective-permute-start(bf16[128,768]{1,0:T(8,128)(2,1)} %bitcast.75), channel_id=1, source_target_pairs={{0,16},{8,24},{16,0},{24,8},{1,17},{9,25},{17,1},{25,9},{2,18},{10... | collective-permute-start | bytes 589832 | tf_op jit(solution)/shard_map/ppermute | solution.py:96
  425.8 3.6 collective-permute-start.6
  426.6 9.1 %collective-permute-start.5 = (bf16[128,384]{1,0:T(8,128)(2,1)S(1)}, bf16[128,384]{1,0:T(8,128)(2,1)S(1)}, u32[]{:S(2)}, u32[]{:S(2)}) collective-permute-start(bf16[128,384]{1,0:T(8,128)(2,1)S(1)} %bitcast.366), channel_id=1, source_target_pairs={{0,16},{8,24},{16,0},{24,8},{1,17},{9,25},{17,1},{25,9},{2,18},{10... | collective-permute-start | bytes 294920 | tf_op jit(solution)/shard_map/ppermute | solution.py:96
  429.4 20.2 %collective-permute-start.12 = (bf16[256,384]{1,0:T(8,128)(2,1)}, bf16[256,384]{1,0:T(8,128)(2,1)}, u32[]{:S(2)}, u32[]{:S(2)}) collective-permute-start(bf16[256,384]{1,0:T(8,128)(2,1)} %get-tuple-element.143), channel_id=1, source_target_pairs={{0,24},{8,16},{16,8},{24,0},{1,25},{9,17},{17,9},{25,1},{2,26},{10... | collective-permute-start | bytes 589832 | tf_op jit(solution)/shard_map/ppermute | solution.py:96
  435.7 13.9 %collective-permute-start.11 = (bf16[256,384]{1,0:T(8,128)(2,1)}, bf16[256,384]{1,0:T(8,128)(2,1)}, u32[]{:S(2)}, u32[]{:S(2)}) collective-permute-start(bf16[256,384]{1,0:T(8,128)(2,1)} %get-tuple-element.142), channel_id=1, source_target_pairs={{0,8},{8,0},{16,24},{24,16},{1,9},{9,1},{17,25},{25,17},{2,10},{10... | collective-permute-start | bytes 589832 | tf_op jit(solution)/shard_map/ppermute | solution.py:96
  436.8 12.8 %collective-permute-start.10 = (bf16[256,384]{1,0:T(8,128)(2,1)}, bf16[256,384]{1,0:T(8,128)(2,1)}, u32[]{:S(2)}, u32[]{:S(2)}) collective-permute-start(bf16[256,384]{1,0:T(8,128)(2,1)} %get-tuple-element.141), channel_id=1, source_target_pairs={{0,16},{8,24},{16,0},{24,8},{1,17},{9,25},{17,1},{25,9},{2,18},{10... | collective-permute-start | bytes 589832 | tf_op jit(solution)/shard_map/ppermute | solution.py:96
  456.1 141.0 %reduce-scatter.15.cloned.1.call-start = ((), (), s32[]{:S(2)}) async-start(), calls=%async_computation.10 | async-start | bytes 2654208
  458.0 9.3 %collective-permute-start.15 = (bf16[128,1216]{0,1:T(8,128)(2,1)S(1)}, bf16[128,1216]{0,1:T(8,128)(2,1)S(1)}, u32[]{:S(2)}, u32[]{:S(2)}) collective-permute-start(bf16[128,1216]{0,1:T(8,128)(2,1)S(1)} %get-tuple-element.137), channel_id=1, source_target_pairs={{0,24},{8,16},{16,8},{24,0},{1,25},{9,17},{17,9},{25,1},{2,26},{10... | collective-permute-start | bytes 933896 | tf_op jit(solution)/shard_map/ppermute | solution.py:96
  459.3 8.0 %collective-permute-start.14 = (bf16[128,1216]{0,1:T(8,128)(2,1)S(1)}, bf16[128,1216]{0,1:T(8,128)(2,1)S(1)}, u32[]{:S(2)}, u32[]{:S(2)}) collective-permute-start(bf16[128,1216]{0,1:T(8,128)(2,1)S(1)} %get-tuple-element.138), channel_id=1, source_target_pairs={{0,8},{8,0},{16,24},{24,16},{1,9},{9,1},{17,25},{25,17},{2,10},{10... | collective-permute-start | bytes 933896 | tf_op jit(solution)/shard_map/ppermute | solution.py:96
  459.6 14.7 %collective-permute-start.13 = (bf16[128,1216]{0,1:T(8,128)(2,1)S(1)}, bf16[128,1216]{0,1:T(8,128)(2,1)S(1)}, u32[]{:S(2)}, u32[]{:S(2)}) collective-permute-start(bf16[128,1216]{0,1:T(8,128)(2,1)S(1)} %get-tuple-element.139), channel_id=1, source_target_pairs={{0,16},{8,24},{16,0},{24,8},{1,17},{9,25},{17,1},{25,9},{2,18},{10... | collective-permute-start | bytes 933896 | tf_op jit(solution)/shard_map/ppermute | solution.py:96
  487.0 170.7 %reduce-scatter.11.cloned.1.call-start = ((), (), s32[]{:S(2)}) async-start(), calls=%async_computation.8 | async-start | bytes 7864320 | tf_op jit(solution)/shard_map/reduce_scatter | solution.py:263
  501.2 8.1 %copy-start.9 = (bf16[768,4,192]{0,2,1:T(8,128)(2,1)S(1)}, bf16[768,4,192]{0,2,1:T(8,128)(2,1)}, u32[]{:S(2)}) copy-start(bf16[768,4,192]{0,2,1:T(8,128)(2,1)} %copy-done.8) | copy-start | bytes 3538948
  501.3 8.5 %copy-start.11 = (bf16[768,4,192]{0,2,1:T(8,128)(2,1)S(1)}, bf16[768,4,192]{0,2,1:T(8,128)(2,1)}, u32[]{:S(2)}) copy-start(bf16[768,4,192]{0,2,1:T(8,128)(2,1)} %copy-done.10) | copy-start | bytes 3538948
  510.2 40.8 %copy-start.99 = (f32[128]{0:T(128)S(1)}, f32[128]{0:T(128)}, u32[]{:S(2)}) copy-start(f32[128]{0:T(128)} %copy-done.98) | copy-start | bytes 1540
  510.2 40.8 %copy-start.60 = (f32[128,768]{1,0:T(8,128)S(1)}, f32[128,768]{1,0:T(8,128)}, u32[]{:S(2)}) copy-start(f32[128,768]{1,0:T(8,128)} %get-tuple-element.118) | copy-start | bytes 1179652
  510.7 41.2 %copy-start.27 = (bf16[768,4,192]{0,2,1:T(8,128)(2,1)S(1)}, bf16[768,4,192]{0,2,1:T(8,128)(2,1)}, u32[]{:S(2)}) copy-start(bf16[768,4,192]{0,2,1:T(8,128)(2,1)} %copy.197) | copy-start | bytes 3538948
  (81 other events, 141.0 us)
Sparse Core Ops, SparseCore 0:
  12.5 130.2 all-gather.5
  144.4 44.5 all-gather.9
  219.3 41.8 all-gather.7
  328.9 63.9 reduce-scatter.8
  456.2 68.4 reduce-scatter.12
  528.0 69.0 reduce-scatter.14
  599.6 58.1 reduce-scatter.10
